TPU v7x, 32 devices: a whole 2x2x4 slice. The times are simulated.
32 devices in a mesh: groups: 2 (over x), heads: 16 (over z, y, core).
Axes of the slice: x: 2, y: 2, z: 4, core: 2. Of those that a mesh axis runs over, the one named last changes fastest.
Arguments:
- tokens: bfloat16 [64, 4, 2304], P('groups'), parts along dimension 0, may hold values from -6 to 6
- qkv_weight: bfloat16 [4608, 12288], P(('groups', 'heads')), parts along dimension 0, may hold values from -0.125 to 0.125
- gate_weight: bfloat16 [4608, 64], P(('groups', 'heads')), parts along dimension 0, may hold values from -0.125 to 0.125
- conv_weight: bfloat16 [8, 12288], P('groups', 'heads'), parts along dimension 0, may hold values from -3 to 3
- delta_state: float32 [64, 32, 128, 128], P(('groups', 'heads')), parts along dimension 0, may hold values from -0.8 to 0.8
- conv_state: float32 [64, 3, 12288], P(('groups', 'heads')), parts along dimension 0, may hold values from -6 to 6
- old_heads: int32 [32], replicated, may hold values from 0 to 31, each once
- new_units: int32 [64], replicated, may hold values from 0 to 63, each once
- slot_of: int32 [64], P('groups'), parts along dimension 0, may hold values from 0 to 31, each once
- lengths: int32 [64], P('groups'), parts along dimension 0, may hold values from 1 to 4, as said below
Outputs:
- readout: bfloat16 [64, 4, 4096], P('groups', None, 'heads'), parts along dimension 0
There are 2 independent parts, one for each index of `groups`. A program takes and returns all parts, laid end to end along the dimension named above; an argument that names none is the same for every part. Nothing has to cross between parts.
Inputs may be any that keep to these rules, and one draw needn't show every extreme that they name: `old_heads`: a permutation of the heads; old column slot p holds head old_heads[p]. `new_units`: a permutation of the head units; unit u is the half u % 2 of the values of head u // 2. `slot_of`: a permutation of the rows. `lengths`: some row decodes all 4 steps and some row only one.
All inputs are finite; a program needn't handle non-finite values.
Results may differ from a plain program's by a relative error of at most 0.001.
Values may be sent and summed in bfloat16 or wider, within the bound.
A program may use at most 128 MiB of HBM per device.

v0:
```python
import jax
import jax.numpy as jnp
from jax import lax
from jax.sharding import PartitionSpec as P

D = 2304
H = 32
DK = 128
TAPS = 4
STEPS = 4
HALF = 64
UNITS = 64
norm_eps = 1e-06


def unit_tables(old_heads, new_units):
    positions = jnp.arange(H, dtype=jnp.int32)
    inverse = jnp.sum(
        jnp.where(old_heads[None, :] == positions[:, None], positions[None, :], 0), axis=1
    )
    heads_of = new_units // 2
    halves = new_units % 2
    old_slots = jnp.sum(
        jnp.where(heads_of[:, None] == positions[None, :], inverse[None, :], 0), axis=1
    )
    return (old_slots, halves)


def select_units(source, selector, halves, precise):
    lead = source.shape[:-1]
    shaped = source.reshape(lead + (3, H, DK))
    if precise:
        picked = jnp.einsum("...mhk,uh->...muk", shaped, selector, precision=lax.Precision.HIGHEST)
    else:
        picked = jnp.einsum(
            "...mhk,uh->...muk", shaped, selector, preferred_element_type=jnp.float32
        ).astype(source.dtype)
    query_part = picked[..., 0, :, :]
    key_part = picked[..., 1, :, :]
    value_full = picked[..., 2, :, :]
    value_part = jnp.where((halves == 0)[:, None], value_full[..., :HALF], value_full[..., HALF:])
    return jnp.concatenate([query_part, key_part, value_part], axis=-1)


def pick_state(delta_state, selector, halves):
    picked = jnp.einsum("rhkv,uh->rukv", delta_state, selector, precision=lax.Precision.HIGHEST)
    return jnp.where((halves == 0)[None, :, None, None], picked[..., :HALF], picked[..., HALF:])


def normalize(values):
    return values * lax.rsqrt(jnp.sum(values * values, axis=-1, keepdims=True) + norm_eps)


def run_steps(projected, gate_pre, history, tap_weights, carried, live_lengths):
    sequence = jnp.concatenate([history, projected], axis=1)
    weights_f = tap_weights.astype(jnp.float32)
    convolved = weights_f[0][None, None] * sequence[:, 0:STEPS]
    for tap_index in range(1, TAPS):
        convolved = (
            convolved
            + weights_f[tap_index][None, None] * sequence[:, tap_index : tap_index + STEPS]
        )
    activated = jax.nn.silu(convolved)
    queries = normalize(activated[..., :DK])
    keys_all = normalize(activated[..., DK : 2 * DK])
    values_all = activated[..., 2 * DK :]
    beta = jax.nn.sigmoid(gate_pre[..., 0])
    decay = jnp.exp(-jax.nn.softplus(gate_pre[..., 1]))
    readouts = []
    for step_index in range(STEPS):
        is_live = (step_index < live_lengths)[:, None, None, None]
        faded = decay[:, step_index, :, None, None] * carried
        predicted = jnp.sum(keys_all[:, step_index, :, :, None] * faded, axis=2)
        updated = (
            faded
            + beta[:, step_index, :, None, None]
            * keys_all[:, step_index, :, :, None]
            * (values_all[:, step_index] - predicted)[:, :, None, :]
        )
        heads_now = jnp.sum(queries[:, step_index, :, :, None] * updated, axis=2)
        carried = jnp.where(is_live, updated, carried)
        readouts.append(jnp.where(is_live[..., 0], heads_now, jnp.zeros_like(heads_now)))
    return jnp.stack(readouts, axis=1).astype(jnp.bfloat16)


def on_device(
    tokens,
    qkv_weight,
    gate_weight,
    conv_weight,
    delta_state,
    conv_state,
    old_heads,
    new_units,
    slot_of,
    lengths,
):
    devices = lax.axis_size("heads")
    my_index = lax.axis_index("heads")
    per_device = UNITS // devices
    unit_width = 2 * DK + HALF
    old_slots, halves = unit_tables(old_heads, new_units)
    head_range = jnp.arange(H, dtype=jnp.int32)
    selector_bits = old_slots[:, None] == head_range[None, :]
    selector_low = selector_bits.astype(jnp.bfloat16)
    selector_full = selector_bits.astype(jnp.float32)
    local_rows = qkv_weight.shape[0]
    packed = select_units(qkv_weight, selector_low, halves, False).reshape(
        local_rows, devices, per_device, unit_width
    )
    gate_shaped = gate_weight.reshape(local_rows, 2, H)
    packed_gate = jnp.einsum(
        "rmh,uh->rum", gate_shaped, selector_low, preferred_element_type=jnp.float32
    ).astype(jnp.bfloat16)
    packed_gate = packed_gate.reshape(local_rows, devices, per_device, 2)
    mine_weight, mine_gate = (
        lax.all_to_all(packed, "heads", split_axis=1, concat_axis=0, tiled=True),
        lax.all_to_all(packed_gate, "heads", split_axis=1, concat_axis=0, tiled=True),
    )
    row_count = tokens.shape[0]
    row_range = jnp.arange(row_count, dtype=jnp.int32)
    match_rows = slot_of[None, :] == row_range[:, None]
    to_old = match_rows.astype(jnp.bfloat16)
    tokens_old = jnp.einsum(
        "ob,bsd->osd", to_old, tokens, preferred_element_type=jnp.float32
    ).astype(jnp.bfloat16)
    lengths_old = jnp.sum(jnp.where(match_rows, lengths[None, :], 0), axis=1)
    flattened = tokens_old.reshape(row_count * STEPS, D)
    projected = jnp.dot(
        flattened,
        mine_weight.reshape(D, per_device * unit_width),
        preferred_element_type=jnp.float32,
    ).reshape(row_count, STEPS, per_device, unit_width)
    gate_pre = jnp.dot(
        flattened, mine_gate.reshape(D, per_device * 2), preferred_element_type=jnp.float32
    ).reshape(row_count, STEPS, per_device, 2)
    taps_all = lax.all_gather(conv_weight, "heads", axis=1, tiled=True)
    tap_table = select_units(taps_all, selector_low, halves, False)
    rows_dev = delta_state.shape[0]
    got_projected, got_gate = (
        lax.all_to_all(projected, "heads", split_axis=0, concat_axis=2, tiled=True),
        lax.all_to_all(gate_pre, "heads", split_axis=0, concat_axis=2, tiled=True),
    )
    live_lengths = lax.dynamic_slice_in_dim(lengths_old, my_index * rows_dev, rows_dev, 0)
    history = select_units(conv_state, selector_full, halves, True)
    carried = pick_state(delta_state, selector_full, halves)
    local_out = run_steps(got_projected, got_gate, history, tap_table, carried, live_lengths)
    outputs_old = lax.all_to_all(local_out, "heads", split_axis=2, concat_axis=0, tiled=True)
    flat_old = outputs_old.reshape(row_count, STEPS, per_device * HALF)
    outputs = jnp.einsum(
        "ob,osc->bsc", to_old, flat_old, preferred_element_type=jnp.float32
    ).astype(jnp.bfloat16)
    return outputs


def solution(mesh):
    in_specs = (
        P("groups", None, None),
        P(("groups", "heads"), None),
        P(("groups", "heads"), None),
        P("groups", "heads"),
        P(("groups", "heads"), None, None, None),
        P(("groups", "heads"), None, None),
        P(),
        P(),
        P("groups"),
        P("groups"),
    )
    out_specs = P("groups", None, "heads")
    return jax.shard_map(
        on_device, mesh=mesh, in_specs=in_specs, out_specs=out_specs, check_vma=False
    )
```

profile of v0, /device:TPU:0, one launch (start us, length us, event | category | flops | bytes accessed | tf_op | source)
XLA Modules:
  0.0 336.9 jit_solution(10728899009877708103)
XLA Ops:
  0.0 0.7 and_select_fusion.1
  0.7 0.7 select_reduce_fusion.1
  1.6 1.0 fusion.9
  2.5 0.7 copy.168
  3.2 7.4 %all-to-all-start.2 = ((bf16[144,16,4,2]{0,3,2,1:T(2,128)(2,1)}), bf16[144,16,4,2]{0,3,2,1:T(2,128)(2,1)S(1)}, u32[]{:S(2)}, u32[]{:S(2)}) async-start(bf16[144,16,4,2]{0,3,2,1:T(2,128)(2,1)} %bitcast.40), calls=%async_computation.2 | async-start | bytes 131072 | tf_op jit(solution)/shard_map/all_to_all | solution.py:118
  10.7 0.7 fusion.50
  11.3 2.7 copy.172
  14.1 2.0 convert_bitcast_fusion
  16.1 2.5 fusion.52
  18.6 0.8 slice_select_fusion.1
  19.4 6.9 %pad_maximum_fusion = bf16[144,16,4,320]{3,2,1,0:T(4,128)(2,1)} fusion(bf16[144,16,4,64]{3,2,1,0:T(4,128)(2,1)S(1)} %bitcast.162, bf16[144,16,4,128]{3,2,1,0:T(4,128)(2,1)S(1)} %bitcast.161, bf16[144,16,4,128]{3,2,1,0:T(4,128)(2,1)S(1)} %bitcast.160), kind=kLoop, calls=%fused_computation.15 | loop fusion | flops 17694720 | bytes 11796480 | tf_op jit(solution)/shard_map/concatenate | solution.py:42
  26.3 9.1 %copy.167 = bf16[144,16,4,320]{3,2,0,1:T(4,128)(2,1)} copy(bf16[144,16,4,320]{3,2,1,0:T(4,128)(2,1)} %pad_maximum_fusion) | data formatting | bytes 11796480 | tf_op jit(solution)/shard_map/concatenate | solution.py:42
  35.4 6.2 %all-to-all-start = ((bf16[144,16,4,320]{3,2,0,1:T(4,128)(2,1)}), bf16[144,16,4,320]{3,2,0,1:T(4,128)(2,1)}, u32[]{:S(2)}, u32[]{:S(2)}) async-start(bf16[144,16,4,320]{3,2,0,1:T(4,128)(2,1)} %copy.167), calls=%async_computation | async-start | bytes 14155776 | tf_op jit(solution)/shard_map/all_to_all | solution.py:117
  41.6 141.3 %all_gather.3 = bf16[4,12288]{1,0:T(4,128)(2,1)S(1)} all-gather(bf16[4,768]{1,0:T(4,128)(2,1)S(1)} %copy-done.3), channel_id=1, replica_groups=mesh['groups'=2,'heads'=16] {'heads'}, dimensions={1}, use_global_device_ids=true | all-gather | bytes 104448 | tf_op jit(solution)/shard_map/all_gather | solution.py:137
  185.4 11.6 %fusion.5 = f32[2,64,128,128]{3,1,2,0:T(8,128)} fusion(f32[2,32,128,128]{3,2,1,0:T(8,128)} %param.14, s32[64]{0:T(128)S(1)} %select_reduce_fusion), kind=kOutput, calls=%fused_computation.21 | convolution fusion | flops 805308416 | bytes 12583168 | tf_op jit(solution)/shard_map/rhkv,uh->rukv/dot_general | solution.py:46
  197.2 0.5 fusion.24
  197.7 0.8 copy.143
  198.5 27.5 %all-to-all-start.3 = ((f32[32,4,4,2]{2,3,1,0:T(2,128)}), f32[32,4,4,2]{2,3,1,0:T(2,128)S(1)}, u32[]{:S(2)}, u32[]{:S(2)}) async-start(f32[32,4,4,2]{2,3,1,0:T(2,128)} %copy.143), calls=%async_computation.3 | async-start | bytes 262144 | tf_op jit(solution)/shard_map/all_to_all | solution.py:142
  226.0 11.9 %reshape.189 = bf16[2304,1280]{1,0:T(8,128)(2,1)} reshape(bf16[16,144,1,4,320]{4,3,1,0,2:T(4,128)(2,1)} %bitcast.24) | data formatting | bytes 11796480 | tf_op jit(solution)/shard_map/reshape | solution.py:131
  237.8 8.9 %copy.135 = bf16[1280,2304]{1,0:T(8,128)(2,1)} copy(bf16[1280,2304]{0,1:T(8,128)(2,1)} %bitcast.158) | data formatting | bytes 11796480 | tf_op jit(solution)/shard_map/dot_general | solution.py:129
  246.7 4.7 %fusion.58 = f32[32,4,4,320]{3,0,2,1:T(8,128)S(1)} fusion(bf16[32,4,2304,1]{2,0,3,1:T(8,128)(2,1)S(1)} %fusion.4, bf16[4,320,2304,1]{2,1,0,3:T(8,128)(2,1)} %bitcast.163), kind=kOutput, calls=%fused_computation.124 | convolution fusion | flops 754974720 | bytes 7143424 | tf_op jit(solution)/shard_map/dot_general | solution.py:129
  251.5 1.4 copy.136
  252.9 6.0 %all-to-all-start.1 = ((f32[32,4,4,320]{3,2,1,0:T(4,128)}), f32[32,4,4,320]{3,2,1,0:T(4,128)S(1)}, u32[]{:S(2)}, u32[]{:S(2)}) async-start(f32[32,4,4,320]{3,2,1,0:T(4,128)} %copy.136), calls=%async_computation.1 | async-start | bytes 1572864 | tf_op jit(solution)/shard_map/all_to_all | solution.py:141
  259.3 18.3 %all-to-all-done.1 = f32[32,4,4,320]{3,2,1,0:T(4,128)S(1)} async-done(((f32[32,4,4,320]{3,2,1,0:T(4,128)}), f32[32,4,4,320]{3,2,1,0:T(4,128)S(1)}, u32[]{:S(2)}, u32[]{:S(2)}) %all-to-all-start.1) | async-done | bytes 655392 | tf_op jit(solution)/shard_map/all_to_all | solution.py:141
  277.8 1.5 divide_multiply_fusion
  282.2 8.5 %multiply_reduce_fusion.7 = (f32[2,64,64]{2,1,0:T(8,128)S(1)}, f32[2,64,128,64]{3,1,2,0:T(8,128)S(1)}) fusion(f32[2,64,128]{1,2,0:T(8,128)S(1)} %copy.148, f32[2,64]{1,0:T(2,128)S(1)} %bitcast.195, f32[2,64,128,128]{3,1,2,0:T(8,128)} %fusion.5, pred[64]{0:T(512)(128)(4,1)S(1)} %fusion.50), kind=kLoop, calls=%fused_computation.12 | loop fusion | flops 4186112 | bytes 12681792 | tf_op jit(solution)/shard_map/reduce_sum | solution.py:73
  290.7 5.1 %multiply_reduce_fusion.5 = f32[2,64,64]{2,1,0:T(8,128)S(1)} fusion(f32[2,64,128,64]{3,1,2,0:T(8,128)S(1)} %get-tuple-element.16, f32[2,64,128]{1,2,0:T(8,128)S(1)} %copy.151, f32[2,64]{1,0:T(2,128)S(1)} %bitcast.202, f32[2,64,64]{2,1,0:T(8,128)S(1)} %sub.35, f32[2,64,128]{1,2,0:T(8,128)S(1)} %copy.147, f32[2,64]{1,0:T(2,128)S(1)} %bitcast.196, ...), kind=kLoop, calls=%fused_computation.9 | loop fusion | flops 7331840 | bytes 4391938 | tf_op jit(solution)/shard_map/reduce_sum | solution.py:73
  295.8 11.4 %multiply_reduce_fusion.6 = (bf16[2,64,64]{2,1,0:T(8,128)(2,1)S(1)}, bf16[2,64,64]{2,1,0:T(8,128)(2,1)S(1)}, f32[2,64,64]{2,1,0:T(8,128)S(1)}, f32[2,64,128,64]{3,1,2,0:T(8,128)S(1)}) fusion(f32[2,64,128,64]{3,1,2,0:T(8,128)S(1)} %get-tuple-element.16, f32[2,64,64]{2,1,0:T(8,128)S(1)} %sub.35, f32[2,64,128]{1,2,0:T(8,128)S(1)} %copy.147, ...), kind=kLoop, calls=%fused_computation.10 | loop fusion | flops 15704064 | bytes 8848900 | tf_op jit(solution)/shard_map/reduce_sum | solution.py:80
  307.3 5.1 %multiply_reduce_fusion.1 = f32[2,64,64]{2,1,0:T(8,128)S(1)} fusion(f32[2,64,128,64]{3,1,2,0:T(8,128)S(1)} %get-tuple-element.18, f32[2,64,128]{1,2,0:T(8,128)S(1)} %copy.157, f32[2,64]{1,0:T(2,128)S(1)} %bitcast.200, f32[2,64,64]{2,1,0:T(8,128)S(1)} %sub.37, f32[2,64,128]{1,2,0:T(8,128)S(1)} %copy.153, f32[2,64]{1,0:T(2,128)S(1)} %bitcast.193, ...), kind=kLoop, calls=%fused_computation.2 | loop fusion | flops 7331840 | bytes 4391938 | tf_op jit(solution)/shard_map/reduce_sum | solution.py:73
  312.4 10.5 %multiply_reduce_fusion.2 = (bf16[2,64,64]{2,1,0:T(8,128)(2,1)S(1)}, bf16[2,64,64]{2,1,0:T(8,128)(2,1)S(1)}) fusion(f32[2,64,128,64]{3,1,2,0:T(8,128)S(1)} %get-tuple-element.18, f32[2,64,64]{2,1,0:T(8,128)S(1)} %sub.37, f32[2,64,128]{1,2,0:T(8,128)S(1)} %copy.153, f32[2,64]{1,0:T(2,128)S(1)} %bitcast.194, f32[2,64,128]{1,2,0:T(8,128)S(1)} %copy.152, ...), kind=kLoop, calls=%fused_computation.4 | loop fusion | flops 11517952 | bytes 4555778 | tf_op jit(solution)/shard_map/reduce_sum | solution.py:80
  323.6 12.1 %all_to_all.81 = bf16[16,2,1024]{2,1,0:T(2,128)(2,1)S(1)} all-to-all(bf16[16,2,1024]{2,1,0:T(2,128)(2,1)S(1)} %reshape.202), channel_id=1, replica_groups=mesh['groups'=2,'heads'=16] {'heads'}, dimensions={0} | all-to-all | bytes 131072 | tf_op jit(solution)/shard_map/all_to_all | solution.py:148
  336.2 0.7 copy.161
  (81 shorter events, 7.0 us)
Async XLA Ops:
  0.0 184.6 %copy-start = (bf16[32,4,2304]{2,1,0:T(4,128)(2,1)S(1)}, bf16[32,4,2304]{2,1,0:T(4,128)(2,1)}, u32[]{:S(2)}) copy-start(bf16[32,4,2304]{2,1,0:T(4,128)(2,1)} %param.10) | copy-start | bytes 1769476
  3.2 32.2 %all-to-all-start.2 = ((bf16[144,16,4,2]{0,3,2,1:T(2,128)(2,1)}), bf16[144,16,4,2]{0,3,2,1:T(2,128)(2,1)S(1)}, u32[]{:S(2)}, u32[]{:S(2)}) async-start(bf16[144,16,4,2]{0,3,2,1:T(2,128)(2,1)} %bitcast.40), calls=%async_computation.2 | async-start | bytes 131072 | tf_op jit(solution)/shard_map/all_to_all | solution.py:118
  35.4 6.2 %copy-start.3 = (bf16[4,768]{1,0:T(4,128)(2,1)S(1)}, bf16[4,768]{1,0:T(4,128)(2,1)}, u32[]{:S(2)}) copy-start(bf16[4,768]{1,0:T(4,128)(2,1)} %param.13) | copy-start | bytes 18436
  35.4 147.6 %copy-start.2 = (f32[2,3,12288]{2,0,1:T(2,128)S(1)}, f32[2,3,12288]{2,0,1:T(2,128)}, u32[]{:S(2)}) copy-start(f32[2,3,12288]{2,0,1:T(2,128)} %param.15) | copy-start | bytes 884740
  35.4 149.0 %copy-start.4 = (s32[32]{0:T(128)S(1)}, s32[32]{0:T(128)}, u32[]{:S(2)}) copy-start(s32[32]{0:T(128)} %param.18) | copy-start | bytes 388
  35.4 149.0 %copy-start.5 = (s32[32]{0:T(128)S(1)}, s32[32]{0:T(128)}, u32[]{:S(2)}) copy-start(s32[32]{0:T(128)} %param.19) | copy-start | bytes 388
  35.4 163.0 %all-to-all-start = ((bf16[144,16,4,320]{3,2,0,1:T(4,128)(2,1)}), bf16[144,16,4,320]{3,2,0,1:T(4,128)(2,1)}, u32[]{:S(2)}, u32[]{:S(2)}) async-start(bf16[144,16,4,320]{3,2,0,1:T(4,128)(2,1)} %copy.167), calls=%async_computation | async-start | bytes 14155776 | tf_op jit(solution)/shard_map/all_to_all | solution.py:117
  198.5 54.4 %all-to-all-start.3 = ((f32[32,4,4,2]{2,3,1,0:T(2,128)}), f32[32,4,4,2]{2,3,1,0:T(2,128)S(1)}, u32[]{:S(2)}, u32[]{:S(2)}) async-start(f32[32,4,4,2]{2,3,1,0:T(2,128)} %copy.143), calls=%async_computation.3 | async-start | bytes 262144 | tf_op jit(solution)/shard_map/all_to_all | solution.py:142
  252.9 24.7 %all-to-all-start.1 = ((f32[32,4,4,320]{3,2,1,0:T(4,128)}), f32[32,4,4,320]{3,2,1,0:T(4,128)S(1)}, u32[]{:S(2)}, u32[]{:S(2)}) async-start(f32[32,4,4,320]{3,2,1,0:T(4,128)} %copy.136), calls=%async_computation.1 | async-start | bytes 1572864 | tf_op jit(solution)/shard_map/all_to_all | solution.py:141
  307.3 29.6 %copy-start.1 = (bf16[32,4,2304]{2,1,0:T(4,128)(2,1)S(1)}, bf16[32,4,2304]{2,1,0:T(4,128)(2,1)}, u32[]{:S(2)}) copy-start(bf16[32,4,2304]{2,1,0:T(4,128)(2,1)} %param.10) | copy-start | bytes 1769476
where the time goes:
time: 338 us; the launch traced here: 337 us
  blocking collectives  153 us (45%)
  other arithmetic  54 us (16%)
  starting transfers between devices  47.1 us (14%)
  local copies, waits for them, and re-layouts  42.4 us (13%)
  matrix products  21.1 us (6%)
  waiting for transfers between devices  18.3 us (5%)
    all_gather x1, blocking collectives, on_device(): taps_all = lax.all_gather(conv_weight, 'heads', axis=1, tiled=True)  141 us
    all_to_all x1, starting transfers between devices, on_device(): lax.all_to_all(gate_pre, 'heads', split_axis=0, concat_axis=2, tiled=True)  27.5 us
    reduce_sum x2, other arithmetic, run_steps(): heads_now = jnp.sum(queries[:, step_index, :, :, None] * updated, axis=2)  22 us
    reduce_sum x3, other arithmetic, run_steps(): predicted = jnp.sum(keys_all[:, step_index, :, :, None] * faded, axis=2)  18.7 us
    all_to_all x1, waiting for transfers between devices, on_device(): lax.all_to_all(projected, 'heads', split_axis=0, concat_axis=2, tiled=True)  18.3 us
    all_to_all x1, blocking collectives, on_device(): lax.all_to_all(local_out, 'heads', split_axis=2, concat_axis=0, tiled=True)  12.1 us
    reshape x1, local copies, waits for them, and re-layouts, on_device(): mine_weight.reshape(D, per_device * unit_width)  11.9 us
    dot_general x1, matrix products, pick_state(): jnp.einsum('rhkv,uh->rukv', delta_state, selector, precision=lax.Precisio...  11.6 us
  transfers between devices with their start and end apart: 4, of which 1 were waited for; matrix products, arithmetic and copies ran while one was open for 20% of the time, Pallas kernels for 0%

commit v1 on v0

--- a/solution.py
+++ b/solution.py
@@ -11,6 +11,13 @@
 HALF = 64
 UNITS = 64
 norm_eps = 1e-06
+
+
+def exchange_blocks(array, axis, split, join):
+    devices = lax.axis_size(axis)
+    blocks = jnp.stack(jnp.split(array, devices, axis=split), axis=0)
+    blocks = lax.all_to_all(blocks, axis, split_axis=0, concat_axis=0)
+    return jnp.concatenate(blocks, axis=join)
 
 
 def unit_tables(old_heads, new_units):
@@ -138,7 +145,7 @@
     tap_table = select_units(taps_all, selector_low, halves, False)
     rows_dev = delta_state.shape[0]
     got_projected, got_gate = (
-        lax.all_to_all(projected, "heads", split_axis=0, concat_axis=2, tiled=True),
+        exchange_blocks(projected, "heads", 0, 2),
         lax.all_to_all(gate_pre, "heads", split_axis=0, concat_axis=2, tiled=True),
     )
     live_lengths = lax.dynamic_slice_in_dim(lengths_old, my_index * rows_dev, rows_dev, 0)

time: 338 us -> 338 us (level)
    dot_general x2 -> x0, local copies, waits for them, and re-layouts: 10.3 us -> none  [on_device(): jnp.dot(flattened, mine_weight.reshape(D, per_device * unit_width), prefe...]
    unnamed x16 -> x31, local copies, waits for them, and re-layouts: 3.04 us -> 12.5 us
where the time goes in v1:
time: 338 us; the launch traced here: 337 us
  blocking collectives  152 us (45%)
  other arithmetic  54 us (16%)
  starting transfers between devices  47.1 us (14%)
  local copies, waits for them, and re-layouts  44.2 us (13%)
  matrix products  20 us (6%)
  waiting for transfers between devices  18.3 us (5%)
    all_gather x1, blocking collectives, on_device(): taps_all = lax.all_gather(conv_weight, 'heads', axis=1, tiled=True)  140 us
    all_to_all x1, starting transfers between devices, on_device(): lax.all_to_all(gate_pre, 'heads', split_axis=0, concat_axis=2, tiled=True)  27.5 us
    reduce_sum x2, other arithmetic, run_steps(): heads_now = jnp.sum(queries[:, step_index, :, :, None] * updated, axis=2)  22 us
    reduce_sum x3, other arithmetic, run_steps(): predicted = jnp.sum(keys_all[:, step_index, :, :, None] * faded, axis=2)  18.7 us
    all_to_all x1, waiting for transfers between devices, exchange_blocks(): blocks = lax.all_to_all(blocks, axis, split_axis=0, concat_axis=0)  18.3 us
    unnamed x31, local copies, waits for them, and re-layouts  12.5 us
    all_to_all x1, blocking collectives, on_device(): lax.all_to_all(local_out, 'heads', split_axis=2, concat_axis=0, tiled=True)  12.1 us
    reshape x1, local copies, waits for them, and re-layouts, on_device(): mine_weight.reshape(D, per_device * unit_width)  11.9 us
  transfers between devices with their start and end apart: 4, of which 1 were waited for; matrix products, arithmetic and copies ran while one was open for 20% of the time, Pallas kernels for 0%

profile of v1, /device:TPU:0, one launch (start us, length us, event | category | flops | bytes accessed | tf_op | source)
XLA Modules:
  0.0 336.6 jit_solution(13988463778477545711)
XLA Ops:
  0.0 0.7 and_select_fusion.1
  0.7 0.7 select_reduce_fusion.1
  1.6 1.0 fusion.8
  2.5 0.7 copy.228
  3.2 7.4 %all-to-all-start.2 = ((bf16[144,16,4,2]{0,3,2,1:T(2,128)(2,1)}), bf16[144,16,4,2]{0,3,2,1:T(2,128)(2,1)S(1)}, u32[]{:S(2)}, u32[]{:S(2)}) async-start(bf16[144,16,4,2]{0,3,2,1:T(2,128)(2,1)} %bitcast.34), calls=%async_computation.2 | async-start | bytes 131072 | tf_op jit(solution)/shard_map/all_to_all | solution.py:125
  10.7 0.7 fusion.50
  11.3 2.7 copy.232
  14.1 2.0 convert_bitcast_fusion
  16.1 2.5 fusion.52
  18.6 0.8 slice_select_fusion.1
  19.4 6.9 %pad_maximum_fusion = bf16[144,16,4,320]{3,2,1,0:T(4,128)(2,1)} fusion(bf16[144,16,4,64]{3,2,1,0:T(4,128)(2,1)S(1)} %bitcast.155, bf16[144,16,4,128]{3,2,1,0:T(4,128)(2,1)S(1)} %bitcast.154, bf16[144,16,4,128]{3,2,1,0:T(4,128)(2,1)S(1)} %bitcast.153), kind=kLoop, calls=%fused_computation.15 | loop fusion | flops 17694720 | bytes 11796480 | tf_op jit(solution)/shard_map/concatenate | solution.py:49
  26.3 9.1 %copy.227 = bf16[144,16,4,320]{3,2,0,1:T(4,128)(2,1)} copy(bf16[144,16,4,320]{3,2,1,0:T(4,128)(2,1)} %pad_maximum_fusion) | data formatting | bytes 11796480 | tf_op jit(solution)/shard_map/concatenate | solution.py:49
  35.4 6.2 %all-to-all-start = ((bf16[144,16,4,320]{3,2,0,1:T(4,128)(2,1)}), bf16[144,16,4,320]{3,2,0,1:T(4,128)(2,1)}, u32[]{:S(2)}, u32[]{:S(2)}) async-start(bf16[144,16,4,320]{3,2,0,1:T(4,128)(2,1)} %copy.227), calls=%async_computation | async-start | bytes 14155776 | tf_op jit(solution)/shard_map/all_to_all | solution.py:124
  42.7 140.3 %all_gather.3 = bf16[4,12288]{1,0:T(4,128)(2,1)S(1)} all-gather(bf16[4,768]{1,0:T(4,128)(2,1)S(1)} %copy-done.3), channel_id=1, replica_groups=mesh['groups'=2,'heads'=16] {'heads'}, dimensions={1}, use_global_device_ids=true | all-gather | bytes 104448 | tf_op jit(solution)/shard_map/all_gather | solution.py:144
  185.0 11.6 %fusion.4 = f32[2,64,128,128]{3,1,2,0:T(8,128)} fusion(f32[2,32,128,128]{3,2,1,0:T(8,128)} %param.14, s32[64]{0:T(128)S(1)} %select_reduce_fusion), kind=kOutput, calls=%fused_computation.20 | convolution fusion | flops 805308416 | bytes 12583168 | tf_op jit(solution)/shard_map/rhkv,uh->rukv/dot_general | solution.py:53
  197.2 0.8 copy.203
  198.0 27.5 %all-to-all-start.3 = ((f32[32,4,4,2]{2,3,1,0:T(2,128)}), f32[32,4,4,2]{2,3,1,0:T(2,128)S(1)}, u32[]{:S(2)}, u32[]{:S(2)}) async-start(f32[32,4,4,2]{2,3,1,0:T(2,128)} %copy.203), calls=%async_computation.3 | async-start | bytes 262144 | tf_op jit(solution)/shard_map/all_to_all | solution.py:149
  225.5 11.9 %reshape.227 = bf16[2304,1280]{1,0:T(8,128)(2,1)} reshape(bf16[16,144,1,4,320]{4,3,1,0,2:T(4,128)(2,1)} %bitcast.22) | data formatting | bytes 11796480 | tf_op jit(solution)/shard_map/reshape | solution.py:138
  237.4 3.6 %fusion.59 = f32[128,1280]{1,0:T(8,128)S(1)} fusion(bf16[128,2304]{1,0:T(8,128)(2,1)S(1)} %reshape.225, bf16[2304,1280]{1,0:T(8,128)(2,1)} %reshape.227), kind=kOutput, calls=%fused_computation.141 | convolution fusion | flops 754974720 | bytes 7143424 | tf_op jit(solution)/shard_map/dot_general | solution.py:136
  243.3 0.6 copy_dynamic-update-slice_fusion.14
  243.9 0.6 copy_dynamic-update-slice_fusion.13
  245.8 0.6 copy_dynamic-update-slice_fusion.10
  252.7 6.0 %all-to-all-start.1 = ((f32[16,2,4,4,320]{4,2,3,1,0:T(4,128)}), f32[16,2,4,4,320]{4,2,3,1,0:T(4,128)S(1)}, u32[]{:S(2)}, u32[]{:S(2)}) async-start(f32[16,2,4,4,320]{4,2,3,1,0:T(4,128)} %copy_dynamic-update-slice_fusion), calls=%async_computation.1 | async-start | bytes 1572864 | tf_op jit(solution)/shard_map/all_to_all | solution.py:19
  259.1 18.3 %all-to-all-done.1 = f32[16,2,4,4,320]{4,2,3,1,0:T(4,128)S(1)} async-done(((f32[16,2,4,4,320]{4,2,3,1,0:T(4,128)}), f32[16,2,4,4,320]{4,2,3,1,0:T(4,128)S(1)}, u32[]{:S(2)}, u32[]{:S(2)}) %all-to-all-start.1) | async-done | bytes 655392 | tf_op jit(solution)/shard_map/all_to_all | solution.py:19
  277.5 1.5 divide_multiply_fusion
  281.9 8.5 %multiply_reduce_fusion.7 = (f32[2,64,64]{2,1,0:T(8,128)S(1)}, f32[2,64,128,64]{3,1,2,0:T(8,128)S(1)}) fusion(f32[2,64,128]{1,2,0:T(8,128)S(1)} %copy.208, f32[2,64]{1,0:T(2,128)S(1)} %bitcast.187, f32[2,64,128,128]{3,1,2,0:T(8,128)} %fusion.4, pred[64]{0:T(512)(128)(4,1)S(1)} %fusion.50), kind=kLoop, calls=%fused_computation.12 | loop fusion | flops 4186112 | bytes 12681792 | tf_op jit(solution)/shard_map/reduce_sum | solution.py:80
  290.4 5.1 %multiply_reduce_fusion.5 = f32[2,64,64]{2,1,0:T(8,128)S(1)} fusion(f32[2,64,128,64]{3,1,2,0:T(8,128)S(1)} %get-tuple-element.16, f32[2,64,128]{1,2,0:T(8,128)S(1)} %copy.211, f32[2,64]{1,0:T(2,128)S(1)} %bitcast.194, f32[2,64,64]{2,1,0:T(8,128)S(1)} %sub.35, f32[2,64,128]{1,2,0:T(8,128)S(1)} %copy.207, f32[2,64]{1,0:T(2,128)S(1)} %bitcast.188, ...), kind=kLoop, calls=%fused_computation.9 | loop fusion | flops 7331840 | bytes 4391938 | tf_op jit(solution)/shard_map/reduce_sum | solution.py:80
  295.5 11.4 %multiply_reduce_fusion.6 = (bf16[2,64,64]{2,1,0:T(8,128)(2,1)S(1)}, bf16[2,64,64]{2,1,0:T(8,128)(2,1)S(1)}, f32[2,64,64]{2,1,0:T(8,128)S(1)}, f32[2,64,128,64]{3,1,2,0:T(8,128)S(1)}) fusion(f32[2,64,128,64]{3,1,2,0:T(8,128)S(1)} %get-tuple-element.16, f32[2,64,64]{2,1,0:T(8,128)S(1)} %sub.35, f32[2,64,128]{1,2,0:T(8,128)S(1)} %copy.207, ...), kind=kLoop, calls=%fused_computation.10 | loop fusion | flops 15704064 | bytes 8848900 | tf_op jit(solution)/shard_map/reduce_sum | solution.py:87
  307.0 5.1 %multiply_reduce_fusion.1 = f32[2,64,64]{2,1,0:T(8,128)S(1)} fusion(f32[2,64,128,64]{3,1,2,0:T(8,128)S(1)} %get-tuple-element.18, f32[2,64,128]{1,2,0:T(8,128)S(1)} %copy.217, f32[2,64]{1,0:T(2,128)S(1)} %bitcast.192, f32[2,64,64]{2,1,0:T(8,128)S(1)} %sub.37, f32[2,64,128]{1,2,0:T(8,128)S(1)} %copy.213, f32[2,64]{1,0:T(2,128)S(1)} %bitcast.185, ...), kind=kLoop, calls=%fused_computation.2 | loop fusion | flops 7331840 | bytes 4391938 | tf_op jit(solution)/shard_map/reduce_sum | solution.py:80
  312.1 10.5 %multiply_reduce_fusion.2 = (bf16[2,64,64]{2,1,0:T(8,128)(2,1)S(1)}, bf16[2,64,64]{2,1,0:T(8,128)(2,1)S(1)}) fusion(f32[2,64,128,64]{3,1,2,0:T(8,128)S(1)} %get-tuple-element.18, f32[2,64,64]{2,1,0:T(8,128)S(1)} %sub.37, f32[2,64,128]{1,2,0:T(8,128)S(1)} %copy.213, f32[2,64]{1,0:T(2,128)S(1)} %bitcast.186, f32[2,64,128]{1,2,0:T(8,128)S(1)} %copy.212, ...), kind=kLoop, calls=%fused_computation.4 | loop fusion | flops 11517952 | bytes 4555778 | tf_op jit(solution)/shard_map/reduce_sum | solution.py:87
  323.3 12.1 %all_to_all.68 = bf16[16,2,1024]{2,1,0:T(2,128)(2,1)S(1)} all-to-all(bf16[16,2,1024]{2,1,0:T(2,128)(2,1)S(1)} %reshape.241), channel_id=1, replica_groups=mesh['groups'=2,'heads'=16] {'heads'}, dimensions={0} | all-to-all | bytes 131072 | tf_op jit(solution)/shard_map/all_to_all | solution.py:155
  335.9 0.7 copy.221
  (114 shorter events, 17.7 us)
Async XLA Ops:
  0.0 41.6 %copy-start = (bf16[32,4,2304]{2,1,0:T(4,128)(2,1)S(1)}, bf16[32,4,2304]{2,1,0:T(4,128)(2,1)}, u32[]{:S(2)}) copy-start(bf16[32,4,2304]{2,1,0:T(4,128)(2,1)} %param.10) | copy-start | bytes 1769476
  3.2 32.2 %all-to-all-start.2 = ((bf16[144,16,4,2]{0,3,2,1:T(2,128)(2,1)}), bf16[144,16,4,2]{0,3,2,1:T(2,128)(2,1)S(1)}, u32[]{:S(2)}, u32[]{:S(2)}) async-start(bf16[144,16,4,2]{0,3,2,1:T(2,128)(2,1)} %bitcast.34), calls=%async_computation.2 | async-start | bytes 131072 | tf_op jit(solution)/shard_map/all_to_all | solution.py:125
  35.4 6.2 %copy-start.4 = (s32[32]{0:T(128)S(1)}, s32[32]{0:T(128)}, u32[]{:S(2)}) copy-start(s32[32]{0:T(128)} %param.18) | copy-start | bytes 388
  35.4 7.3 %copy-start.3 = (bf16[4,768]{1,0:T(4,128)(2,1)S(1)}, bf16[4,768]{1,0:T(4,128)(2,1)}, u32[]{:S(2)}) copy-start(bf16[4,768]{1,0:T(4,128)(2,1)} %param.13) | copy-start | bytes 18436
  35.4 147.6 %copy-start.2 = (f32[2,3,12288]{2,0,1:T(2,128)S(1)}, f32[2,3,12288]{2,0,1:T(2,128)}, u32[]{:S(2)}) copy-start(f32[2,3,12288]{2,0,1:T(2,128)} %param.15) | copy-start | bytes 884740
  35.4 149.0 %copy-start.5 = (s32[32]{0:T(128)S(1)}, s32[32]{0:T(128)}, u32[]{:S(2)}) copy-start(s32[32]{0:T(128)} %param.19) | copy-start | bytes 388
  35.4 162.6 %all-to-all-start = ((bf16[144,16,4,320]{3,2,0,1:T(4,128)(2,1)}), bf16[144,16,4,320]{3,2,0,1:T(4,128)(2,1)}, u32[]{:S(2)}, u32[]{:S(2)}) async-start(bf16[144,16,4,320]{3,2,0,1:T(4,128)(2,1)} %copy.227), calls=%async_computation | async-start | bytes 14155776 | tf_op jit(solution)/shard_map/all_to_all | solution.py:124
  198.0 54.7 %all-to-all-start.3 = ((f32[32,4,4,2]{2,3,1,0:T(2,128)}), f32[32,4,4,2]{2,3,1,0:T(2,128)S(1)}, u32[]{:S(2)}, u32[]{:S(2)}) async-start(f32[32,4,4,2]{2,3,1,0:T(2,128)} %copy.203), calls=%async_computation.3 | async-start | bytes 262144 | tf_op jit(solution)/shard_map/all_to_all | solution.py:149
  252.7 24.7 %all-to-all-start.1 = ((f32[16,2,4,4,320]{4,2,3,1,0:T(4,128)}), f32[16,2,4,4,320]{4,2,3,1,0:T(4,128)S(1)}, u32[]{:S(2)}, u32[]{:S(2)}) async-start(f32[16,2,4,4,320]{4,2,3,1,0:T(4,128)} %copy_dynamic-update-slice_fusion), calls=%async_computation.1 | async-start | bytes 1572864 | tf_op jit(solution)/shard_map/all_to_all | solution.py:19
  307.0 29.6 %copy-start.1 = (bf16[32,4,2304]{2,1,0:T(4,128)(2,1)S(1)}, bf16[32,4,2304]{2,1,0:T(4,128)(2,1)}, u32[]{:S(2)}) copy-start(bf16[32,4,2304]{2,1,0:T(4,128)(2,1)} %param.10) | copy-start | bytes 1769476
